TPU v7x, 32 devices: a whole 2x2x4 slice. The times are simulated.
32 devices in a mesh: grp: 4 (over y, x), line: 8 (over z, core).
Axes of the slice: x: 2, y: 2, z: 4, core: 2. Of those that a mesh axis runs over, the one named last changes fastest.
Arguments:
- velocity: bfloat16 [3, 1536, 96, 512], P(None, 'line', 'grp'), may hold values from -6 to 6
- vorticity: bfloat16 [3, 1536, 96, 512], P(None, 'line', 'grp'), may hold values from -6 to 6
- wall_velocity: float32 [2, 256, 96, 1536], P(None, ('grp', 'line')), may hold values from -6 to 6
- wall_vorticity: float32 [2, 256, 96, 1536], P(None, ('grp', 'line')), may hold values from -6 to 6
- keep_mask: int32 [256, 96], P(('grp', 'line')), may hold values from 0 to 1, as said below
- derivative_band: float32 [7, 1536], replicated, may hold values from -3 to 3
- eigenvalues: float32 [1536], replicated, may hold values from 0.25 to 4
- eigenbasis: float32 [1536, 1536], replicated, may hold values from -0.15625 to 0.15625
Outputs:
- new_velocity: float32 [2, 256, 96, 1536], P(None, ('grp', 'line'))
- new_vorticity: float32 [2, 256, 96, 1536], P(None, ('grp', 'line'))
Inputs may be any that keep to these rules, and one draw needn't show every extreme that they name: keep_mask is 0 wherever kx >= 170, or 32 <= kz < 64.
All inputs are finite; a program needn't handle non-finite values.
Results may differ from a plain program's by a relative error of at most 0.0003.
Values sent between devices are 32-bit elements; how exact they have to be, the bound alone decides.
A program may use at most 384 MiB of HBM per device.

v0:
```python
import math
import jax
import jax.numpy as jnp
from jax import lax
from jax.sharding import PartitionSpec as P

HIGHEST_PRECISION = lax.Precision.HIGHEST


def phase_table(indices, points):
    index_cols = jnp.arange(points, dtype=jnp.int32)[None, :]
    phase_angle = (indices[:, None] * index_cols % points).astype(jnp.float32) * (
        2.0 * math.pi / points
    )
    norm_scale = 1.0 / math.sqrt(points)
    return (jnp.cos(phase_angle) * norm_scale, jnp.sin(phase_angle) * norm_scale)


def signed_wave(indices, points):
    signed_index = jnp.where(indices < points // 2, indices, indices - points)
    return signed_index.astype(jnp.float32) / (points / 2.0)


def curl_terms(spectra, stream_wave, span_wave):
    slope_source = jnp.stack(
        [
            -stream_wave * spectra[0, 1] - span_wave * spectra[2, 1],
            stream_wave * spectra[0, 0] + span_wave * spectra[2, 0],
        ]
    )
    normal_term = jnp.stack(
        [
            -span_wave * spectra[0, 1] + stream_wave * spectra[2, 1],
            span_wave * spectra[0, 0] - stream_wave * spectra[2, 0],
        ]
    )
    return (slope_source, normal_term)


def banded(padded, band_rows, extent):
    summed = band_rows[0] * padded[..., 0:extent]
    for offset in range(1, 7):
        summed = summed + band_rows[offset] * padded[..., offset : offset + extent]
    return summed


def local(
    velocity,
    vorticity,
    wall_velocity,
    wall_vorticity,
    keep_mask,
    derivative_band,
    eigenvalues,
    eigenbasis,
):
    group_count = lax.axis_size("grp")
    line_count = lax.axis_size("line")
    group_index = lax.axis_index("grp")
    line_index = lax.axis_index("line")
    moving = velocity.astype(jnp.float32)
    turning = vorticity.astype(jnp.float32)
    lamb_vector = jnp.stack(
        [
            moving[1] * turning[2] - moving[2] * turning[1],
            moving[2] * turning[0] - moving[0] * turning[2],
            moving[0] * turning[1] - moving[1] * turning[0],
        ]
    )
    slab_depth = lamb_vector.shape[1]
    span_share = lamb_vector.shape[2]
    stream_points = lamb_vector.shape[3]
    span_points = span_share * group_count
    stream_modes = stream_points // 2
    group_modes = stream_modes // group_count
    line_modes = group_modes // line_count
    span_keep = span_points // 3
    wall_points = wall_velocity.shape[3]
    span_list = jnp.concatenate(
        [
            jnp.arange(span_keep, dtype=jnp.int32),
            jnp.arange(span_points - span_keep, span_points, dtype=jnp.int32),
        ]
    )
    span_count = span_list.shape[0]
    stream_cosine, stream_sine = phase_table(
        jnp.arange(stream_modes, dtype=jnp.int32), stream_points
    )
    stream_table = jnp.stack(
        [
            stream_cosine.reshape(group_count, group_modes, stream_points),
            -stream_sine.reshape(group_count, group_modes, stream_points),
        ],
        1,
    )
    stream_table = stream_table.reshape(2 * stream_modes, stream_points)
    stream_spectra = jnp.einsum(
        "rx,cx->rc",
        lamb_vector.reshape(-1, stream_points),
        stream_table,
        precision=HIGHEST_PRECISION,
    )
    stream_spectra = stream_spectra.reshape(3, slab_depth, span_share, 2 * stream_modes)
    span_cosine, span_sine = phase_table(span_list, span_points)
    planes = lax.all_to_all(stream_spectra, "grp", split_axis=3, concat_axis=2, tiled=True)
    count_items = planes.shape[1]
    cosine_part = jnp.einsum("qz,fnzc->fcqn", span_cosine, planes, precision=HIGHEST_PRECISION)
    sine_part = jnp.einsum("qz,fnzc->fcqn", span_sine, planes, precision=HIGHEST_PRECISION)
    cosine_part = cosine_part.reshape(3, 2, group_modes, span_count, count_items)
    sine_part = sine_part.reshape(3, 2, group_modes, span_count, count_items)
    real_part = cosine_part[:, 0] + sine_part[:, 1]
    imag_part = cosine_part[:, 1] - sine_part[:, 0]
    local_modes = jnp.stack([real_part, imag_part], 1)
    span_wave = signed_wave(span_list, span_points)[:, None]
    device_modes = (group_index * line_count + line_index) * line_modes + jnp.arange(
        line_modes, dtype=jnp.int32
    )
    device_wave = (device_modes.astype(jnp.float32) / stream_modes)[:, None, None]
    whole_lines = lax.all_to_all(local_modes, "line", split_axis=2, concat_axis=4, tiled=True)
    wave_square = device_wave * device_wave + span_wave * span_wave
    slope_source, normal_term = curl_terms(whole_lines, device_wave, span_wave)
    padded = jnp.pad(slope_source, ((0, 0), (0, 0), (0, 0), (3, 3)))
    arrived = jnp.stack(
        [wave_square * whole_lines[1] - banded(padded, derivative_band, wall_points), normal_term]
    )
    middle = jnp.zeros((2, 2, line_modes, span_points - 2 * span_keep, wall_points), jnp.float32)
    arrived = jnp.concatenate(
        [arrived[:, :, :, :span_keep], middle, arrived[:, :, :, span_keep:]], 3
    )
    keep_weight = keep_mask.astype(jnp.float32)[:, :, None]
    right_side = jnp.stack([wall_velocity, wall_vorticity]) + keep_weight * arrived
    full_wave = signed_wave(jnp.arange(span_points, dtype=jnp.int32), span_points)[:, None]
    full_square = device_wave * device_wave + full_wave * full_wave
    eigen_coeffs = jnp.einsum(
        "fpkqy,yj->fpkqj", right_side, eigenbasis, precision=HIGHEST_PRECISION
    )
    eigen_coeffs = eigen_coeffs / (eigenvalues + full_square)
    solved = jnp.einsum("fpkqj,yj->fpkqy", eigen_coeffs, eigenbasis, precision=HIGHEST_PRECISION)
    return (solved[0], solved[1])


def solution(mesh):
    placed = (
        P(None, "line", "grp", None),
        P(None, "line", "grp", None),
        P(None, ("grp", "line"), None, None),
        P(None, ("grp", "line"), None, None),
        P(("grp", "line"), None),
        P(),
        P(),
        P(),
    )
    return jax.shard_map(
        local,
        mesh=mesh,
        in_specs=placed,
        out_specs=(P(None, ("grp", "line"), None, None), P(None, ("grp", "line"), None, None)),
        check_vma=False,
    )
```

profile of v0, /device:TPU:0, one launch (start us, length us, event | category | flops | bytes accessed | tf_op | source)
XLA Modules:
  0.0 1655.5 jit_solution(10274515562087793496)
XLA Ops:
  0.7 17.1 %convert_element_type.71 = f32[3,192,24,512]{3,2,1,0:T(8,128)} convert(bf16[3,192,24,512]{3,2,1,0:T(8,128)(2,1)} %param.8) | non-fusion elementwise | flops 7077888 | bytes 42467328 | tf_op jit(solution)/shard_map/convert_element_type | solution.py:61
  20.1 10.3 convert_element_type.72
  32.6 30.8 %multiply_subtract_fusion.2 = (f32[1,192,24,512]{3,2,1,0:T(8,128)}, f32[1,192,24,512]{3,2,1,0:T(8,128)}, f32[1,192,24,512]{3,2,1,0:T(8,128)}) fusion(f32[3,192,24,512]{3,2,1,0:T(8,128)} %convert_element_type.72, f32[3,192,24,512]{3,2,1,0:T(8,128)} %convert_element_type.71), kind=kLoop, calls=%fused_computation.37 | loop fusion | flops 21233664 | bytes 84934656 | tf_op jit(solution)/shard_map/sub | solution.py:65
  63.5 51.6 %fusion = f32[3,192,24,512]{3,2,1,0:T(8,128)} fusion(f32[512,512,1,1]{1,0,3,2:T(8,128)S(1)} %bitcast.85, f32[1,192,24,512]{3,2,1,0:T(8,128)} %get-tuple-element.14, f32[1,192,24,512]{3,2,1,0:T(8,128)} %get-tuple-element.13, f32[1,192,24,512]{3,2,1,0:T(8,128)} %get-tuple-element.12), kind=kOutput, calls=%fused_computation | convolution fusion | flops 43500699648 | bytes 57671680 | tf_op jit(solution)/shard_map/rx,cx->rc/dot_general | solution.py:97
  115.1 36.9 %copy.28 = f32[3,192,24,512]{1,2,0,3:T(8,128)} copy(f32[3,192,24,512]{3,2,1,0:T(8,128)} %fusion) | data formatting | bytes 56623104 | tf_op jit(solution)/shard_map/rx,cx->rc/dot_general | solution.py:97
  152.0 11.0 all-to-all-start
  163.1 408.4 %all-to-all-done = f32[3,192,24,512]{1,2,0,3:T(8,128)} async-done(((f32[3,192,24,512]{1,2,0,3:T(8,128)}), f32[3,192,24,512]{1,2,0,3:T(8,128)}, u32[]{:S(2)}, u32[]{:S(2)}) %all-to-all-start) | async-done | bytes 28311584 | tf_op jit(solution)/shard_map/all_to_all | solution.py:105
  571.6 34.4 %copy.29 = f32[3,192,24,4,128]{4,2,3,1,0:T(8,128)} copy(f32[3,192,24,4,128]{1,2,0,4,3:T(8,128)} %bitcast.5) | data formatting | bytes 56623104 | tf_op jit(solution)/shard_map/all_to_all | solution.py:105
  606.0 26.2 %convolution_bitcast_fusion.1 = f32[3,128,64,192]{1,2,3,0:T(8,128)} fusion(f32[3,192,96,128]{3,2,1,0:T(8,128)} %bitcast.80, s32[64]{0:T(128)S(1)} %get-tuple-element.11), kind=kOutput, calls=%fused_computation.40 | convolution fusion | flops 5435879424 | bytes 47186176 | tf_op jit(solution)/shard_map/qz,fnzc->fcqn/dot_general | solution.py:107
  632.3 26.2 %convolution_bitcast_fusion = f32[3,128,64,192]{1,2,3,0:T(8,128)} fusion(f32[3,192,96,128]{3,2,1,0:T(8,128)} %bitcast.81, s32[64]{0:T(128)S(1)} %get-tuple-element.11), kind=kOutput, calls=%fused_computation.39 | convolution fusion | flops 5435879424 | bytes 47186176 | tf_op jit(solution)/shard_map/qz,fnzc->fcqn/dot_general | solution.py:108
  658.4 25.1 %copy.30 = f32[3,128,64,192]{3,2,1,0:T(8,128)} copy(f32[3,128,64,192]{1,2,3,0:T(8,128)} %convolution_bitcast_fusion.1) | data formatting | bytes 37748736 | tf_op jit(solution)/shard_map/qz,fnzc->fcqn/transpose | solution.py:107
  683.5 25.1 %copy.31 = f32[3,128,64,192]{3,2,1,0:T(8,128)} copy(f32[3,128,64,192]{1,2,3,0:T(8,128)} %convolution_bitcast_fusion) | data formatting | bytes 37748736 | tf_op jit(solution)/shard_map/qz,fnzc->fcqn/transpose | solution.py:108
  708.6 27.5 %slice_add_fusion = (f32[3,1,64,64,192]{4,3,2,1,0:T(8,128)}, f32[3,1,64,64,192]{4,3,2,1,0:T(8,128)}) fusion(f32[3,2,64,64,192]{4,3,2,1,0:T(8,128)} %bitcast.83, f32[3,2,64,64,192]{4,3,2,1,0:T(8,128)} %bitcast.82), kind=kLoop, calls=%fused_computation.24 | loop fusion | flops 4718592 | bytes 56623104 | tf_op jit(solution)/shard_map/add | solution.py:111
  736.1 9.4 pad_maximum_fusion
  763.7 540.4 %all-to-all-done.1 = f32[3,2,64,64,192]{4,3,1,0,2:T(8,128)} async-done(((f32[3,2,64,64,192]{4,3,1,0,2:T(8,128)}), f32[3,2,64,64,192]{4,3,1,0,2:T(8,128)}, u32[]{:S(2)}, u32[]{:S(2)}) %all-to-all-start.1) | async-done | bytes 18874400 | tf_op jit(solution)/shard_map/all_to_all | solution.py:119
  1304.1 26.5 %copy.35 = f32[3,2,8,64,8,192]{5,4,3,2,1,0:T(8,128)} copy(f32[3,2,8,64,8,192]{5,3,1,0,2,4:T(8,128)} %bitcast.20) | data formatting | bytes 37748736 | tf_op jit(solution)/shard_map/all_to_all | solution.py:119
  1330.7 25.3 %all_to_all.33 = f32[3,2,8,64,1536]{4,3,2,1,0:T(8,128)} reshape(f32[3,2,8,64,8,192]{5,4,3,2,1,0:T(8,128)} %copy.35) | data formatting | bytes 37748736 | tf_op jit(solution)/shard_map/all_to_all | solution.py:119
  1355.9 17.5 %copy.33 = f32[3,2,64,64,192]{4,3,2,1,0:T(8,128)} copy(f32[3,2,64,64,192]{4,3,1,0,2:T(8,128)} %all-to-all-done.1) | data formatting | bytes 37748736 | tf_op jit(solution)/shard_map/all_to_all | solution.py:119
  1377.5 9.9 copy.34
  1387.4 9.5 squeeze.14
  1408.8 23.5 %subtract_bitcast_fusion = f32[1,2,8,64,1536]{4,3,2,1,0:T(8,128)} fusion(f32[2,8,64,1536]{3,2,1,0:T(8,128)} %pad_maximum_fusion.1, f32[2,8,64,1536]{3,2,1,0:T(8,128)} %squeeze.14, f32[1536]{0:T(1024)S(1)} %get-tuple-element.7, f32[1536]{0:T(1024)S(1)} %get-tuple-element.8, f32[1536]{0:T(1024)S(1)} %get-tuple-element.3, f32[1536]{0:T(1024)S(1)} %get-tuple-element.4, ...), kind=kLoop, calls=%fused_computation.44 | loop fusion | flops 23592960 | bytes 18919424 | tf_op jit(solution)/shard_map/stack | solution.py:123
  1438.6 105.2 %fusion.9 = f32[2,2,8,96,1536]{4,3,2,1,0:T(8,128)} fusion(f32[1,2,8,64,1536]{4,3,2,1,0:T(8,128)} %maximum_bitcast_fusion, f32[1,2,8,64,1536]{4,3,2,1,0:T(8,128)} %subtract_bitcast_fusion, f32[1,2,8,96,1536]{4,3,2,1,0:T(8,128)} %bitcast.86, f32[1,2,8,96,1536]{4,3,2,1,0:T(8,128)} %bitcast.87, f32[2,2,8,32,1536]{4,3,2,1,0:T(8,128)} %fusion.28, ...), kind=kOutput, calls=%fused_computation.11 | convolution fusion | flops 87015555072 | bytes 66063744 | tf_op jit(solution)/shard_map/fpkqy,yj->fpkqj/dot_general | solution.py:134
  1543.8 99.0 %fusion.19 = f32[2,2,8,96,1536]{4,3,2,1,0:T(8,128)} fusion(f32[2,2,8,96,1536]{4,3,2,1,0:T(8,128)} %fusion.9, f32[1536,1536]{1,0:T(8,128)} %param.15, f32[8,96,1536]{2,1,0:T(8,128)} %broadcast_add_fusion), kind=kOutput, calls=%fused_computation.21 | convolution fusion | flops 86977806336 | bytes 51904512 | tf_op jit(solution)/shard_map/fpkqj,yj->fpkqy/dot_general | solution.py:138
  1642.7 12.6 slice_bitcast_fusion
  (32 shorter events, 45.0 us)
Async XLA Ops:
  0.6 19.5 %copy-start = (bf16[3,192,24,512]{3,2,1,0:T(8,128)(2,1)S(1)}, bf16[3,192,24,512]{3,2,1,0:T(8,128)(2,1)}, u32[]{:S(2)}) copy-start(bf16[3,192,24,512]{3,2,1,0:T(8,128)(2,1)} %param.9) | copy-start | bytes 42467332
  152.0 419.6 %all-to-all-start = ((f32[3,192,24,512]{1,2,0,3:T(8,128)}), f32[3,192,24,512]{1,2,0,3:T(8,128)}, u32[]{:S(2)}, u32[]{:S(2)}) async-start(f32[3,192,24,512]{1,2,0,3:T(8,128)} %copy.28), calls=%async_computation | async-start | bytes 75497472 | tf_op jit(solution)/shard_map/all_to_all | solution.py:105
  754.2 6.6 copy-start.3
  754.2 6.7 copy-start.1
  754.2 7.0 copy-start.2
  754.2 550.0 %all-to-all-start.1 = ((f32[3,2,64,64,192]{4,3,1,0,2:T(8,128)}), f32[3,2,64,64,192]{4,3,1,0,2:T(8,128)}, u32[]{:S(2)}, u32[]{:S(2)}) async-start(f32[3,2,64,64,192]{4,3,1,0,2:T(8,128)} %copy.32), calls=%async_computation.1 | async-start | bytes 50331648 | tf_op jit(solution)/shard_map/all_to_all | solution.py:119
where the time goes:
time: 1660 us
  waiting for transfers between devices  949 us (57%)
  matrix products  308 us (19%)
  local copies, waits for them, and re-layouts  238 us (14%)
  other arithmetic  142 us (9%)
  starting transfers between devices  17.6 us (1%)
    all_to_all x1, waiting for transfers between devices, local(): lax.all_to_all(local_modes, 'line', split_axis=2, concat_axis=4, tiled=True)  540 us
    all_to_all x1, waiting for transfers between devices, local(): lax.all_to_all(stream_spectra, 'grp', split_axis=3, concat_axis=2, tiled=...  408 us
    dot_general x1, matrix products, local(): jnp.einsum('fpkqy,yj->fpkqj', right_side, eigenbasis, precision=HIGHEST_P...  105 us
    dot_general x1, matrix products, local(): jnp.einsum('fpkqj,yj->fpkqy', eigen_coeffs, eigenbasis, precision=HIGHEST...  99 us
    all_to_all x3, local copies, waits for them, and re-layouts, local(): lax.all_to_all(local_modes, 'line', split_axis=2, concat_axis=4, tiled=True)  69.3 us
    dot_general x1, matrix products, local(): jnp.einsum('rx,cx->rc', lamb_vector.reshape(-1, stream_points), stream_ta...  51.6 us
    dot_general x1, local copies, waits for them, and re-layouts, local(): jnp.einsum('rx,cx->rc', lamb_vector.reshape(-1, stream_points), stream_ta...  36.9 us
    all_to_all x1, local copies, waits for them, and re-layouts, local(): lax.all_to_all(stream_spectra, 'grp', split_axis=3, concat_axis=2, tiled=...  34.4 us
  transfers between devices with their start and end apart: 2, of which 2 were waited for; matrix products, arithmetic and copies ran while one was open for 0% of the time, Pallas kernels for 0%

commit v1 on v0

--- a/solution.py
+++ b/solution.py
@@ -1,3 +1,4 @@
+import functools
 import math
 import jax
 import jax.numpy as jnp
@@ -5,6 +6,31 @@
 from jax.sharding import PartitionSpec as P
 
 HIGHEST_PRECISION = lax.Precision.HIGHEST
+
+
+def sides_connect(u, device_axis, k_dim, array_axis):
+    big, built = (lax.axis_size(device_axis), lax.axis_index(device_axis))
+    piece_out = u.shape[k_dim] // big
+    reached = list(u.shape)
+    reached[k_dim] = piece_out
+    formed = reached[array_axis]
+    reached[array_axis] = formed * big
+    field_out = jnp.zeros(reached, u.dtype)
+    for jj in tuple(range(big)):
+        state_next = lax.dynamic_slice_in_dim(u, (built ^ jj) * piece_out, piece_out, axis=k_dim)
+        if jj:
+            state_next = lax.ppermute(
+                state_next,
+                axis_name=device_axis,
+                perm=tuple(((dev, dev ^ jj) for dev in range(big))),
+            )
+        field_out = lax.dynamic_update_slice_in_dim(
+            field_out, state_next, (built ^ jj) * formed, axis=array_axis
+        )
+    return field_out
+
+
+press_heaps = functools.partial(sides_connect, device_axis="line", k_dim=2, array_axis=4)
 
 
 def phase_table(indices, points):
@@ -116,7 +142,7 @@
         line_modes, dtype=jnp.int32
     )
     device_wave = (device_modes.astype(jnp.float32) / stream_modes)[:, None, None]
-    whole_lines = lax.all_to_all(local_modes, "line", split_axis=2, concat_axis=4, tiled=True)
+    whole_lines = press_heaps(local_modes)
     wave_square = device_wave * device_wave + span_wave * span_wave
     slope_source, normal_term = curl_terms(whole_lines, device_wave, span_wave)
     padded = jnp.pad(slope_source, ((0, 0), (0, 0), (0, 0), (3, 3)))

time: 1660 us -> 1580 us (0.952)
  the two profiles are of different devices: /device:TPU:0 before, /device:TPU:16 now
where the time goes in v1:
time: 1580 us; the launch traced here: 1570 us
  waiting for transfers between devices  805 us (51%)
  matrix products  308 us (19%)
  local copies, waits for them, and re-layouts  289 us (18%)
  other arithmetic  151 us (10%)
  starting transfers between devices  16.1 us (1%)
    all_to_all x1, waiting for transfers between devices, local(): lax.all_to_all(stream_spectra, 'grp', split_axis=3, concat_axis=2, tiled=...  407 us
    ppermute x7, waiting for transfers between devices, sides_connect(): lax.ppermute(state_next, axis_name=device_axis, perm=tuple(((dev, dev ^ j...  398 us
    dynamic_update_slice x8, local copies, waits for them, and re-layouts, sides_connect(): lax.dynamic_update_slice_in_dim(field_out, state_next, (built ^ jj) * for...  144 us
    dot_general x1, matrix products, local(): jnp.einsum('fpkqy,yj->fpkqj', right_side, eigenbasis, precision=HIGHEST_P...  105 us
    dot_general x1, matrix products, local(): jnp.einsum('fpkqj,yj->fpkqy', eigen_coeffs, eigenbasis, precision=HIGHEST...  99.2 us
    dot_general x1, matrix products, local(): jnp.einsum('rx,cx->rc', lamb_vector.reshape(-1, stream_points), stream_ta...  51.5 us
    dot_general x1, local copies, waits for them, and re-layouts, local(): jnp.einsum('rx,cx->rc', lamb_vector.reshape(-1, stream_points), stream_ta...  36.8 us
    all_to_all x1, local copies, waits for them, and re-layouts, local(): lax.all_to_all(stream_spectra, 'grp', split_axis=3, concat_axis=2, tiled=...  34.4 us
  transfers between devices with their start and end apart: 8, of which 6 were waited for; matrix products, arithmetic and copies ran while one was open for 9% of the time, Pallas kernels for 0%

profile of v1, /device:TPU:16, one launch (start us, length us, event | category | flops | bytes accessed | tf_op | source)
XLA Modules:
  0.0 1570.3 jit_solution(15877060042743950831)
XLA Ops:
  0.7 17.1 %convert_element_type.71 = f32[3,192,24,512]{3,2,1,0:T(8,128)} convert(bf16[3,192,24,512]{3,2,1,0:T(8,128)(2,1)} %param.8) | non-fusion elementwise | flops 7077888 | bytes 42467328 | tf_op jit(solution)/shard_map/convert_element_type | solution.py:87
  32.6 30.8 %multiply_subtract_fusion.2 = (f32[1,192,24,512]{3,2,1,0:T(8,128)}, f32[1,192,24,512]{3,2,1,0:T(8,128)}, f32[1,192,24,512]{3,2,1,0:T(8,128)}) fusion(f32[3,192,24,512]{3,2,1,0:T(8,128)} %convert_element_type.72, f32[3,192,24,512]{3,2,1,0:T(8,128)} %convert_element_type.71), kind=kLoop, calls=%fused_computation.52 | loop fusion | flops 21233664 | bytes 84934656 | tf_op jit(solution)/shard_map/sub | solution.py:91
  63.5 51.5 %fusion = f32[3,192,24,512]{3,2,1,0:T(8,128)} fusion(f32[512,512,1,1]{1,0,3,2:T(8,128)S(1)} %bitcast.84, f32[1,192,24,512]{3,2,1,0:T(8,128)} %get-tuple-element.14, f32[1,192,24,512]{3,2,1,0:T(8,128)} %get-tuple-element.13, f32[1,192,24,512]{3,2,1,0:T(8,128)} %get-tuple-element.12), kind=kOutput, calls=%fused_computation.16 | convolution fusion | flops 43500699648 | bytes 57671680 | tf_op jit(solution)/shard_map/rx,cx->rc/dot_general | solution.py:123
  115.1 36.8 %copy.22 = f32[3,192,24,512]{1,2,0,3:T(8,128)} copy(f32[3,192,24,512]{3,2,1,0:T(8,128)} %fusion) | data formatting | bytes 56623104 | tf_op jit(solution)/shard_map/rx,cx->rc/dot_general | solution.py:123
  163.0 407.0 %all-to-all-done = f32[3,192,24,512]{1,2,0,3:T(8,128)} async-done(((f32[3,192,24,512]{1,2,0,3:T(8,128)}), f32[3,192,24,512]{1,2,0,3:T(8,128)}, u32[]{:S(2)}, u32[]{:S(2)}) %all-to-all-start) | async-done | bytes 28311584 | tf_op jit(solution)/shard_map/all_to_all | solution.py:131
  570.0 34.4 %copy.23 = f32[3,192,24,4,128]{4,2,3,1,0:T(8,128)} copy(f32[3,192,24,4,128]{1,2,0,4,3:T(8,128)} %bitcast.5) | data formatting | bytes 56623104 | tf_op jit(solution)/shard_map/all_to_all | solution.py:131
  604.4 26.2 %convolution_bitcast_fusion.1 = f32[3,128,64,192]{1,2,3,0:T(8,128)} fusion(f32[3,192,96,128]{3,2,1,0:T(8,128)} %bitcast.80, s32[64]{0:T(128)S(1)} %get-tuple-element.11), kind=kOutput, calls=%fused_computation.55 | convolution fusion | flops 5435879424 | bytes 47186176 | tf_op jit(solution)/shard_map/qz,fnzc->fcqn/dot_general | solution.py:133
  630.7 26.2 %convolution_bitcast_fusion = f32[3,128,64,192]{1,2,3,0:T(8,128)} fusion(f32[3,192,96,128]{3,2,1,0:T(8,128)} %bitcast.81, s32[64]{0:T(128)S(1)} %get-tuple-element.11), kind=kOutput, calls=%fused_computation.54 | convolution fusion | flops 5435879424 | bytes 47186176 | tf_op jit(solution)/shard_map/qz,fnzc->fcqn/dot_general | solution.py:134
  656.8 25.1 %copy.24 = f32[3,128,64,192]{3,2,1,0:T(8,128)} copy(f32[3,128,64,192]{1,2,3,0:T(8,128)} %convolution_bitcast_fusion.1) | data formatting | bytes 37748736 | tf_op jit(solution)/shard_map/qz,fnzc->fcqn/transpose | solution.py:133
  681.9 25.1 %copy.25 = f32[3,128,64,192]{3,2,1,0:T(8,128)} copy(f32[3,128,64,192]{1,2,3,0:T(8,128)} %convolution_bitcast_fusion) | data formatting | bytes 37748736 | tf_op jit(solution)/shard_map/qz,fnzc->fcqn/transpose | solution.py:134
  707.0 27.5 %slice_subtract_fusion = (f32[3,1,64,64,192]{4,3,2,1,0:T(8,128)}, f32[3,1,64,64,192]{4,3,2,1,0:T(8,128)}) fusion(f32[3,2,64,64,192]{4,3,2,1,0:T(8,128)} %bitcast.83, f32[3,2,64,64,192]{4,3,2,1,0:T(8,128)} %bitcast.82), kind=kLoop, calls=%fused_computation.38 | loop fusion | flops 4718592 | bytes 56623104 | tf_op jit(solution)/shard_map/sub | solution.py:138
  757.8 191.0 %collective-permute-done.1 = f32[3,2,8,64,192]{4,3,2,1,0:T(8,128)} collective-permute-done((f32[3,2,8,64,192]{4,3,2,1,0:T(8,128)}, f32[3,2,8,64,192]{4,3,2,1,0:T(8,128)}, u32[]{:S(2)}, u32[]{:S(2)}) %collective-permute-start.1) | collective-permute-done | bytes 2359328 | tf_op jit(solution)/shard_map/ppermute | solution.py:22
  975.9 20.3 %dynamic_update_slice.25 = f32[3,2,8,64,1536]{4,3,2,1,0:T(8,128)} dynamic-update-slice(f32[3,2,8,64,1536]{4,3,2,1,0:T(8,128)} %dynamic_update_slice.24, f32[3,2,8,64,192]{4,3,2,1,0:T(8,128)} %collective-permute-done, s32[]{:T(128)} %constant.75.clone.1, s32[]{:T(128)} %constant.75.clone.1, s32[]{:T(128)} %constant.75.clone.1, s32[]{:T(128)} %constant.75.clone.1, s32[]{:T(128)S(6)} %select_n.107) | dynamic-update-slice | bytes 4718596 | tf_op jit(solution)/shard_map/dynamic_update_slice | solution.py:27
  1015.6 19.6 %dynamic_update_slice.27 = f32[3,2,8,64,1536]{4,3,2,1,0:T(8,128)} dynamic-update-slice(f32[3,2,8,64,1536]{4,3,2,1,0:T(8,128)} %dynamic_update_slice.26, f32[3,2,8,64,192]{4,3,2,1,0:T(8,128)} %collective-permute-done.2, s32[]{:T(128)} %constant.75.clone.1, s32[]{:T(128)} %constant.75.clone.1, s32[]{:T(128)} %constant.75.clone.1, s32[]{:T(128)} %constant.75.clone.1, s32[]{:T(128)S(6)} %select_n.111) | dynamic-update-slice | bytes 4718596 | tf_op jit(solution)/shard_map/dynamic_update_slice | solution.py:27
  1035.2 16.0 %dynamic_update_slice.28 = f32[3,2,8,64,1536]{4,3,2,1,0:T(8,128)} dynamic-update-slice(f32[3,2,8,64,1536]{4,3,2,1,0:T(8,128)} %dynamic_update_slice.27, f32[3,2,8,64,192]{4,3,2,1,0:T(8,128)} %collective-permute-done.3, s32[]{:T(128)} %constant.75.clone.1, s32[]{:T(128)} %constant.75.clone.1, s32[]{:T(128)} %constant.75.clone.1, s32[]{:T(128)} %constant.75.clone.1, s32[]{:T(128)S(6)} %select_n.113) | dynamic-update-slice | bytes 4718596 | tf_op jit(solution)/shard_map/dynamic_update_slice | solution.py:27
  1051.2 103.1 %collective-permute-done.4 = f32[3,2,8,64,192]{4,3,2,1,0:T(8,128)} collective-permute-done((f32[3,2,8,64,192]{4,3,2,1,0:T(8,128)}, f32[3,2,8,64,192]{4,3,2,1,0:T(8,128)}, u32[]{:S(2)}, u32[]{:S(2)}) %collective-permute-start.4) | collective-permute-done | bytes 2359328 | tf_op jit(solution)/shard_map/ppermute | solution.py:22
  1154.2 20.4 %dynamic_update_slice.29 = f32[3,2,8,64,1536]{4,3,2,1,0:T(8,128)} dynamic-update-slice(f32[3,2,8,64,1536]{4,3,2,1,0:T(8,128)} %dynamic_update_slice.28, f32[3,2,8,64,192]{4,3,2,1,0:T(8,128)} %collective-permute-done.4, s32[]{:T(128)} %constant.75.clone.1, s32[]{:T(128)} %constant.75.clone.1, s32[]{:T(128)} %constant.75.clone.1, s32[]{:T(128)} %constant.75.clone.1, s32[]{:T(128)S(6)} %select_n.115) | dynamic-update-slice | bytes 4718596 | tf_op jit(solution)/shard_map/dynamic_update_slice | solution.py:27
  1174.6 50.3 %collective-permute-done.5 = f32[3,2,8,64,192]{4,3,2,1,0:T(8,128)} collective-permute-done((f32[3,2,8,64,192]{4,3,2,1,0:T(8,128)}, f32[3,2,8,64,192]{4,3,2,1,0:T(8,128)}, u32[]{:S(2)}, u32[]{:S(2)}) %collective-permute-start.5) | collective-permute-done | bytes 2359328 | tf_op jit(solution)/shard_map/ppermute | solution.py:22
  1224.9 16.0 %dynamic_update_slice.30 = f32[3,2,8,64,1536]{4,3,2,1,0:T(8,128)} dynamic-update-slice(f32[3,2,8,64,1536]{4,3,2,1,0:T(8,128)} %dynamic_update_slice.29, f32[3,2,8,64,192]{4,3,2,1,0:T(8,128)} %collective-permute-done.5, s32[]{:T(128)} %constant.75.clone.1, s32[]{:T(128)} %constant.75.clone.1, s32[]{:T(128)} %constant.75.clone.1, s32[]{:T(128)} %constant.75.clone.1, s32[]{:T(128)S(6)} %select_n.117) | dynamic-update-slice | bytes 4718596 | tf_op jit(solution)/shard_map/dynamic_update_slice | solution.py:27
  1240.9 50.2 %collective-permute-done.6 = f32[3,2,8,64,192]{4,3,2,1,0:T(8,128)} collective-permute-done((f32[3,2,8,64,192]{4,3,2,1,0:T(8,128)}, f32[3,2,8,64,192]{4,3,2,1,0:T(8,128)}, u32[]{:S(2)}, u32[]{:S(2)}) %collective-permute-start.6) | collective-permute-done | bytes 2359328 | tf_op jit(solution)/shard_map/ppermute | solution.py:22
  1291.1 20.4 %dynamic_update_slice.31 = f32[3,2,8,64,1536]{4,3,2,1,0:T(8,128)} dynamic-update-slice(f32[3,2,8,64,1536]{4,3,2,1,0:T(8,128)} %dynamic_update_slice.30, f32[3,2,8,64,192]{4,3,2,1,0:T(8,128)} %collective-permute-done.6, s32[]{:T(128)} %constant.75.clone.1, s32[]{:T(128)} %constant.75.clone.1, s32[]{:T(128)} %constant.75.clone.1, s32[]{:T(128)} %constant.75.clone.1, s32[]{:T(128)S(6)} %select_n.119) | dynamic-update-slice | bytes 4718596 | tf_op jit(solution)/shard_map/dynamic_update_slice | solution.py:27
  1323.4 23.4 %fusion.31 = f32[1,2,8,64,1536]{4,3,2,1,0:T(8,128)} fusion(f32[3,2,8,64,1536]{4,3,2,1,0:T(8,128)} %dynamic_update_slice.31, f32[2,8,64,1536]{3,2,1,0:T(8,128)} %pad_maximum_fusion, f32[1536]{0:T(1024)S(1)} %get-tuple-element.7, f32[1536]{0:T(1024)S(1)} %get-tuple-element.8, f32[1536]{0:T(1024)S(1)} %get-tuple-element.3, f32[1536]{0:T(1024)S(1)} %get-tuple-element.4, ...), kind=kLoop, calls=%fused_computation.60 | loop fusion | flops 23592960 | bytes 18919424 | tf_op jit(solution)/shard_map/stack | solution.py:149
  1353.1 104.9 %fusion.9 = f32[2,2,8,96,1536]{4,3,2,1,0:T(8,128)} fusion(f32[1,2,8,64,1536]{4,3,2,1,0:T(8,128)} %maximum_bitcast_fusion, f32[1,2,8,64,1536]{4,3,2,1,0:T(8,128)} %fusion.31, f32[1,2,8,96,1536]{4,3,2,1,0:T(8,128)} %bitcast.85, f32[1,2,8,96,1536]{4,3,2,1,0:T(8,128)} %bitcast.86, f32[2,2,8,32,1536]{4,3,2,1,0:T(8,128)} %fusion.28, f32[96]{0:T(128)S(1)} %pad.6.clone, ...), kind=kOutput, calls=%fused_computation.26 | convolution fusion | flops 87015555072 | bytes 66063744 | tf_op jit(solution)/shard_map/fpkqy,yj->fpkqj/dot_general | solution.py:160
  1458.0 99.2 %fusion.19 = f32[2,2,8,96,1536]{4,3,2,1,0:T(8,128)} fusion(f32[2,2,8,96,1536]{4,3,2,1,0:T(8,128)} %fusion.9, f32[1536,1536]{1,0:T(8,128)} %param.15, f32[8,96,1536]{2,1,0:T(8,128)} %broadcast_add_fusion), kind=kOutput, calls=%fused_computation.36 | convolution fusion | flops 86977806336 | bytes 51904512 | tf_op jit(solution)/shard_map/fpkqj,yj->fpkqy/dot_general | solution.py:164
  (47 shorter events, 126.5 us)
Async XLA Ops:
  0.6 19.5 %copy-start = (bf16[3,192,24,512]{3,2,1,0:T(8,128)(2,1)S(1)}, bf16[3,192,24,512]{3,2,1,0:T(8,128)(2,1)}, u32[]{:S(2)}) copy-start(bf16[3,192,24,512]{3,2,1,0:T(8,128)(2,1)} %param.9) | copy-start | bytes 42467332
  151.9 418.1 %all-to-all-start = ((f32[3,192,24,512]{1,2,0,3:T(8,128)}), f32[3,192,24,512]{1,2,0,3:T(8,128)}, u32[]{:S(2)}, u32[]{:S(2)}) async-start(f32[3,192,24,512]{1,2,0,3:T(8,128)} %copy.22), calls=%async_computation | async-start | bytes 75497472 | tf_op jit(solution)/shard_map/all_to_all | solution.py:131
  746.1 11.1 collective-permute-start
  746.2 202.5 %collective-permute-start.1 = (f32[3,2,8,64,192]{4,3,2,1,0:T(8,128)}, f32[3,2,8,64,192]{4,3,2,1,0:T(8,128)}, u32[]{:S(2)}, u32[]{:S(2)}) collective-permute-start(f32[3,2,8,64,192]{4,3,2,1,0:T(8,128)} %get-tuple-element.20), channel_id=1, source_target_pairs={{0,2},{1,3},{2,0},{3,1},{4,6},{5,7},{6,4},{7,5},{8,10},{9,11},{10,... | collective-permute-start | bytes 7077896 | tf_op jit(solution)/shard_map/ppermute | solution.py:22
  747.9 267.7 %collective-permute-start.2 = (f32[3,2,8,64,192]{4,3,2,1,0:T(8,128)}, f32[3,2,8,64,192]{4,3,2,1,0:T(8,128)}, u32[]{:S(2)}, u32[]{:S(2)}) collective-permute-start(f32[3,2,8,64,192]{4,3,2,1,0:T(8,128)} %get-tuple-element.21), channel_id=1, source_target_pairs={{0,3},{1,2},{2,1},{3,0},{4,7},{5,6},{6,5},{7,4},{8,11},{9,10},{10,... | collective-permute-start | bytes 7077896 | tf_op jit(solution)/shard_map/ppermute | solution.py:22
  748.1 200.8 %copy-start.3 = (s32[8,96]{1,0:T(8,128)S(1)}, s32[8,96]{1,0:T(8,128)}, u32[]{:S(2)}) copy-start(s32[8,96]{1,0:T(8,128)} %param.12) | copy-start | bytes 9220
  748.1 200.9 %copy-start.1 = (f32[7,1536]{1,0:T(8,128)S(1)}, f32[7,1536]{1,0:T(8,128)}, u32[]{:S(2)}) copy-start(f32[7,1536]{1,0:T(8,128)} %param.13) | copy-start | bytes 129028
  748.1 201.2 %copy-start.2 = (f32[1536]{0:T(1024)S(1)}, f32[1536]{0:T(1024)}, u32[]{:S(2)}) copy-start(f32[1536]{0:T(1024)} %param.14) | copy-start | bytes 18436
  748.1 287.1 %collective-permute-start.3 = (f32[3,2,8,64,192]{4,3,2,1,0:T(8,128)}, f32[3,2,8,64,192]{4,3,2,1,0:T(8,128)}, u32[]{:S(2)}, u32[]{:S(2)}) collective-permute-start(f32[3,2,8,64,192]{4,3,2,1,0:T(8,128)} %get-tuple-element.22), channel_id=1, source_target_pairs={{0,4},{1,5},{2,6},{3,7},{4,0},{5,1},{6,2},{7,3},{8,12},{9,13},{10,... | collective-permute-start | bytes 7077896 | tf_op jit(solution)/shard_map/ppermute | solution.py:22
  754.9 399.4 %collective-permute-start.4 = (f32[3,2,8,64,192]{4,3,2,1,0:T(8,128)}, f32[3,2,8,64,192]{4,3,2,1,0:T(8,128)}, u32[]{:S(2)}, u32[]{:S(2)}) collective-permute-start(f32[3,2,8,64,192]{4,3,2,1,0:T(8,128)} %get-tuple-element.24), channel_id=1, source_target_pairs={{0,5},{1,4},{2,7},{3,6},{4,1},{5,0},{6,3},{7,2},{8,13},{9,12},{10,... | collective-permute-start | bytes 7077896 | tf_op jit(solution)/shard_map/ppermute | solution.py:22
  757.3 467.7 %collective-permute-start.5 = (f32[3,2,8,64,192]{4,3,2,1,0:T(8,128)}, f32[3,2,8,64,192]{4,3,2,1,0:T(8,128)}, u32[]{:S(2)}, u32[]{:S(2)}) collective-permute-start(f32[3,2,8,64,192]{4,3,2,1,0:T(8,128)} %get-tuple-element.23), channel_id=1, source_target_pairs={{0,6},{1,7},{2,4},{3,5},{4,2},{5,3},{6,0},{7,1},{8,14},{9,15},{10,... | collective-permute-start | bytes 7077896 | tf_op jit(solution)/shard_map/ppermute | solution.py:22
  948.7 342.4 %collective-permute-start.6 = (f32[3,2,8,64,192]{4,3,2,1,0:T(8,128)}, f32[3,2,8,64,192]{4,3,2,1,0:T(8,128)}, u32[]{:S(2)}, u32[]{:S(2)}) collective-permute-start(f32[3,2,8,64,192]{4,3,2,1,0:T(8,128)} %get-tuple-element.17), channel_id=1, source_target_pairs={{0,7},{1,6},{2,5},{3,4},{4,3},{5,2},{6,1},{7,0},{8,15},{9,14},{10,... | collective-permute-start | bytes 7077896 | tf_op jit(solution)/shard_map/ppermute | solution.py:22
